TPU v7x, 32 devices: a whole 2x2x4 slice. The times are simulated.
32 devices in a mesh: section: 4 (over x, core), tp: 8 (over z, y).
Axes of the slice: x: 2, y: 2, z: 4, core: 2. Of those that a mesh axis runs over, the one named last changes fastest.
Arguments:
- patches: bfloat16 [2, 32, 4096], P(None, None, 'tp'), may hold values from -6 to 6
- table_ids: int32 [2, 32], replicated, may hold values from 0 to 32767
- lengths: int32 [2, 2], replicated, may hold values from 16 to 32
- embed_table: bfloat16 [32768, 4096], P('section', 'tp'), may hold values from -6 to 6
- norm_gain: bfloat16 [4, 4096], P('section'), may hold values from 0.099609375 to 1.8984375
- w_query: bfloat16 [4, 4096, 4096], P('section', None, 'tp'), may hold values from -0.09375 to 0.09375
- w_key: bfloat16 [4, 4096, 4096], P('section', None, 'tp'), may hold values from -0.09375 to 0.09375
- w_value: bfloat16 [4, 4096, 4096], P('section', None, 'tp'), may hold values from -0.09375 to 0.09375
- w_out: bfloat16 [4, 4096, 4096], P('section', None, 'tp'), may hold values from -0.09375 to 0.09375
Outputs:
- layer_rows: bfloat16 [4, 2, 32, 4096], P('section', None, None, 'tp')
Inputs may be any that keep to these rules, and one draw needn't show every extreme that they name: `lengths`: column 0 counts a micro-batch's valid patches, column 1 its valid table tokens.
All inputs are finite; a program needn't handle non-finite values.
Results may differ from a plain program's by a relative error of at most 0.01.
Values may be sent and summed in bfloat16 or wider, within the bound.
No kernel may reach another device: no remote copies, remote signals or barrier semaphores. Data moves between devices by JAX's collectives and lax.ppermute only.
A program may use at most 64 MiB of HBM per device.

v0:
```python
import math
import jax
import jax.numpy as jnp
from jax import lax
from jax.sharding import PartitionSpec as P

HEADS = 32
epsilon = 1e-06


def shifted(block, axis, distance):
    devices = range(lax.axis_size(axis))
    route = [(i - distance, i) for i in devices if i - distance in devices]
    return lax.ppermute(block, axis, route)


def local(patches, table_ids, lengths, embed_table, norm_gain, w_query, w_key, w_value, w_out):
    section_count = lax.axis_size("section")
    section_index = lax.axis_index("section")
    is_encoder = section_index < section_count // 2
    micro_count, row_count, width_local = patches.shape
    width_full = w_query.shape[1]
    head_dim = width_full // HEADS
    heads_local = width_local // head_dim
    score_scale = 1.0 / math.sqrt(head_dim)
    query_weight = w_query[0]
    key_weight = w_key[0]
    value_weight = w_value[0]
    out_weight = w_out[0]
    gain_row = norm_gain[0].astype(jnp.float32)
    vocab_local = embed_table.shape[0]
    local_ids = table_ids.reshape(-1) - section_index * vocab_local
    vocab_cols = lax.broadcasted_iota(jnp.int32, (local_ids.shape[0], vocab_local), 1)
    one_hot = (local_ids[:, None] == vocab_cols).astype(jnp.bfloat16)
    looked_up = jnp.dot(one_hot, embed_table, preferred_element_type=jnp.float32)
    embedded = lax.psum(looked_up.astype(jnp.bfloat16), "section")
    embedded = embedded.reshape(micro_count, row_count, width_local)
    first_inputs = jnp.concatenate([patches, embedded], axis=1)
    query_pos = lax.broadcasted_iota(jnp.int32, (row_count, 2 * row_count), 0)
    key_pos = lax.broadcasted_iota(jnp.int32, (row_count, 2 * row_count), 1)

    def head_outputs(full_rows, batch_index):
        values_f = full_rows.astype(jnp.float32)
        inverse = lax.rsqrt(jnp.mean(values_f * values_f, axis=-1, keepdims=True) + epsilon)
        normed = (values_f * inverse * gain_row).astype(jnp.bfloat16)
        own_rows = jnp.where(is_encoder, normed[:row_count], normed[row_count:])
        query = (
            jnp.dot(own_rows, query_weight, preferred_element_type=jnp.float32) * score_scale
        ).astype(jnp.bfloat16)
        key_rows = jnp.dot(normed, key_weight, preferred_element_type=jnp.float32).astype(
            jnp.bfloat16
        )
        value_rows = jnp.dot(normed, value_weight, preferred_element_type=jnp.float32).astype(
            jnp.bfloat16
        )
        query_heads = query.reshape(row_count, heads_local, head_dim)
        key_heads = key_rows.reshape(2 * row_count, heads_local, head_dim)
        value_heads = value_rows.reshape(2 * row_count, heads_local, head_dim)
        scores = jnp.einsum(
            "qhd,khd->hqk", query_heads, key_heads, preferred_element_type=jnp.float32
        )
        patch_count = lengths[batch_index, 0]
        table_count = lengths[batch_index, 1]
        patch_mask = (key_pos < row_count) & (key_pos < patch_count)
        table_mask = (
            (key_pos >= row_count)
            & (key_pos - row_count <= query_pos)
            & (key_pos - row_count < table_count)
        )
        key_mask = jnp.where(is_encoder, patch_mask, patch_mask | table_mask)
        exp_scores = jnp.where(key_mask[None], jnp.exp(scores), 0.0)
        weights = (exp_scores / jnp.sum(exp_scores, axis=-1, keepdims=True)).astype(jnp.bfloat16)
        head_mix = jnp.einsum(
            "hqk,khd->qhd", weights, value_heads, preferred_element_type=jnp.float32
        )
        return head_mix.astype(jnp.bfloat16).reshape(row_count, width_local)

    def add_block(piece):
        return jnp.dot(piece, out_weight, preferred_element_type=jnp.float32)

    def project_heads(head_mix):
        return add_block(lax.all_gather(head_mix, "tp", axis=1, tiled=True))

    def pass_on(stream):
        return shifted(stream, "section", 1)

    def place_rows(stream, updated):
        with_patches = jnp.concatenate([updated, stream[row_count:]], axis=0)
        with_table = jnp.concatenate([stream[:row_count], updated], axis=0)
        return jnp.where(is_encoder, with_patches, with_table)

    stash = jnp.zeros((micro_count, row_count, width_local), jnp.bfloat16)
    step_count = micro_count + section_count - 1

    def advance(step_index, carry):
        incoming, stash_rows = carry
        batch_index = step_index - section_index
        active = (batch_index >= 0) & (batch_index < micro_count)
        batch_index = jnp.clip(batch_index, 0, micro_count - 1)
        first_input = lax.dynamic_index_in_dim(first_inputs, batch_index, 0, keepdims=False)
        stream = jnp.where(section_index == 0, first_input, incoming)
        full_rows = lax.all_gather(stream, "tp", axis=1, tiled=True)
        change = project_heads(head_outputs(full_rows, batch_index))
        residual = jnp.where(is_encoder, stream[:row_count], stream[row_count:])
        updated = (residual.astype(jnp.float32) + change).astype(jnp.bfloat16)
        stored = lax.dynamic_update_index_in_dim(stash_rows, updated, batch_index, 0)
        stash_rows = jnp.where(active, stored, stash_rows)
        return (pass_on(place_rows(stream, updated)), stash_rows)

    start_stream = jnp.zeros((2 * row_count, width_local), jnp.bfloat16)
    final_carry = lax.fori_loop(0, step_count, advance, (start_stream, stash))
    return final_carry[1][None]


def solution(mesh):
    return jax.shard_map(
        local,
        mesh=mesh,
        in_specs=(
            P(None, None, "tp"),
            P(),
            P(),
            P("section", "tp"),
            P("section", None),
            P("section", None, "tp"),
            P("section", None, "tp"),
            P("section", None, "tp"),
            P("section", None, "tp"),
        ),
        out_specs=P("section", None, None, "tp"),
        check_vma=False,
    )
```

profile of v0, /device:TPU:1, one launch (start us, length us, event | category | flops | bytes accessed | tf_op | source)
XLA Modules:
  0.0 446.4 jit_solution(11587463912320818533)
XLA Ops:
  7.3 5.7 %fusion.32 = bf16[64,512]{1,0:T(8,128)(2,1)} fusion(bf16[8192,512]{1,0:T(8,128)(2,1)} %param.14, s32[64]{0:T(128)S(1)} %sub.33), kind=kOutput, calls=%fused_computation.52 | convolution fusion | flops 537427968 | bytes 8454400 | tf_op jit(solution)/shard_map/dot_general | solution.py:35
  13.0 32.2 %all-reduce.2.cloned.1.call-done = bf16[2,32,512]{2,1,0:T(8,128)(2,1)} async-done(((bf16[2,32,512]{2,1,0:T(8,128)(2,1)}), bf16[2,32,512]{2,1,0:T(8,128)(2,1)}) %all-reduce.2.cloned.1.call-update) | async-done | bytes 65552 | tf_op jit(solution)/shard_map/psum | solution.py:36
  45.3 0.8 pad_maximum_fusion
  46.2 392.8 %while.19 = (s32[]{:T(128)}, bf16[64,512]{1,0:T(8,128)(2,1)S(1)}, bf16[2,32,512]{2,1,0:T(8,128)(2,1)S(1)}, pred[]{:T(512)}, pred[]{:T(512)}, /*index=5*/s32[]{:T...) while((s32[]{:T(128)}, bf16[64,512]{1,0:T(8,128)(2,1)S(1)}, ...), condition=%wide.region_4.5_spmd.clone.clone, body=%wide.region_1.4_spmd.clone.clone.sunk | while | flops 812038400 | bytes 56055120 | solution.py:111
  46.2 25.8 %all_gather.26 = bf16[64,4096]{1,0:T(8,128)(2,1)S(1)} all-gather(bf16[64,512]{1,0:T(8,128)(2,1)S(1)} %bitcast_select_fusion.3), channel_id=1, replica_groups=mesh['section'=4,'tp'=8] {'tp'}, dimensions={1}, use_global_device_ids=true | all-gather | bytes 589824 | tf_op jit(solution)/shard_map/while/body/eval_jaxpr/all_gather | solution.py:102
  73.0 3.2 fusion.79
  76.2 0.8 fusion.78
  77.1 0.8 fusion.80
  77.9 1.2 or_select_fusion.2
  79.5 24.6 %all_gather.27 = bf16[32,4096]{1,0:T(8,128)(2,1)S(1)} all-gather(bf16[32,512]{1,0:T(8,128)(2,1)S(1)} %bitcast.89), channel_id=1, replica_groups=mesh['section'=4,'tp'=8] {'tp'}, dimensions={1}, use_global_device_ids=true | all-gather | bytes 294912 | tf_op jit(solution)/shard_map/while/body/eval_jaxpr/all_gather | solution.py:82
  104.1 3.0 fusion.83
  107.2 15.9 %collective-permute-start = (bf16[64,512]{1,0:T(8,128)(2,1)S(1)}, bf16[64,512]{1,0:T(8,128)(2,1)S(1)}, u32[]{:S(2)}, u32[]{:S(2)}) collective-permute-start(bf16[64,512]{1,0:T(8,128)(2,1)S(1)} %maximum_select_fusion.2), channel_id=1, source_target_pairs={{0,8},{8,16},{16,24},{1,9},{9,17},{17,25},{2,10},{10,18},{18,26},{... | collective-permute-start | bytes 196616 | tf_op jit(solution)/shard_map/while/body/eval_jaxpr/ppermute | solution.py:14
  123.1 1.3 collective-permute-done
  124.4 25.8 %all_gather.26 = bf16[64,4096]{1,0:T(8,128)(2,1)S(1)} all-gather(bf16[64,512]{1,0:T(8,128)(2,1)S(1)} %bitcast_select_fusion.3), channel_id=1, replica_groups=mesh['section'=4,'tp'=8] {'tp'}, dimensions={1}, use_global_device_ids=true | all-gather | bytes 589824 | tf_op jit(solution)/shard_map/while/body/eval_jaxpr/all_gather | solution.py:102
  151.2 3.2 fusion.79
  154.4 0.8 fusion.78
  155.2 0.8 fusion.80
  156.0 1.2 or_select_fusion.2
  157.7 24.6 %all_gather.27 = bf16[32,4096]{1,0:T(8,128)(2,1)S(1)} all-gather(bf16[32,512]{1,0:T(8,128)(2,1)S(1)} %bitcast.89), channel_id=1, replica_groups=mesh['section'=4,'tp'=8] {'tp'}, dimensions={1}, use_global_device_ids=true | all-gather | bytes 294912 | tf_op jit(solution)/shard_map/while/body/eval_jaxpr/all_gather | solution.py:82
  182.3 3.0 fusion.83
  185.3 16.4 %collective-permute-start = (bf16[64,512]{1,0:T(8,128)(2,1)S(1)}, bf16[64,512]{1,0:T(8,128)(2,1)S(1)}, u32[]{:S(2)}, u32[]{:S(2)}) collective-permute-start(bf16[64,512]{1,0:T(8,128)(2,1)S(1)} %maximum_select_fusion.2), channel_id=1, source_target_pairs={{0,8},{8,16},{16,24},{1,9},{9,17},{17,25},{2,10},{10,18},{18,26},{... | collective-permute-start | bytes 196616 | tf_op jit(solution)/shard_map/while/body/eval_jaxpr/ppermute | solution.py:14
  201.7 1.3 collective-permute-done
  203.1 25.5 %all_gather.26 = bf16[64,4096]{1,0:T(8,128)(2,1)S(1)} all-gather(bf16[64,512]{1,0:T(8,128)(2,1)S(1)} %bitcast_select_fusion.3), channel_id=1, replica_groups=mesh['section'=4,'tp'=8] {'tp'}, dimensions={1}, use_global_device_ids=true | all-gather | bytes 589824 | tf_op jit(solution)/shard_map/while/body/eval_jaxpr/all_gather | solution.py:102
  229.6 3.2 fusion.79
  232.8 0.8 fusion.78
  233.6 0.8 fusion.80
  234.4 1.2 or_select_fusion.2
  236.1 24.5 %all_gather.27 = bf16[32,4096]{1,0:T(8,128)(2,1)S(1)} all-gather(bf16[32,512]{1,0:T(8,128)(2,1)S(1)} %bitcast.89), channel_id=1, replica_groups=mesh['section'=4,'tp'=8] {'tp'}, dimensions={1}, use_global_device_ids=true | all-gather | bytes 294912 | tf_op jit(solution)/shard_map/while/body/eval_jaxpr/all_gather | solution.py:82
  260.6 3.0 fusion.83
  263.7 16.6 %collective-permute-start = (bf16[64,512]{1,0:T(8,128)(2,1)S(1)}, bf16[64,512]{1,0:T(8,128)(2,1)S(1)}, u32[]{:S(2)}, u32[]{:S(2)}) collective-permute-start(bf16[64,512]{1,0:T(8,128)(2,1)S(1)} %maximum_select_fusion.2), channel_id=1, source_target_pairs={{0,8},{8,16},{16,24},{1,9},{9,17},{17,25},{2,10},{10,18},{18,26},{... | collective-permute-start | bytes 196616 | tf_op jit(solution)/shard_map/while/body/eval_jaxpr/ppermute | solution.py:14
  280.3 1.3 collective-permute-done
  281.6 25.5 %all_gather.26 = bf16[64,4096]{1,0:T(8,128)(2,1)S(1)} all-gather(bf16[64,512]{1,0:T(8,128)(2,1)S(1)} %bitcast_select_fusion.3), channel_id=1, replica_groups=mesh['section'=4,'tp'=8] {'tp'}, dimensions={1}, use_global_device_ids=true | all-gather | bytes 589824 | tf_op jit(solution)/shard_map/while/body/eval_jaxpr/all_gather | solution.py:102
  308.2 3.2 fusion.79
  311.4 0.8 fusion.78
  312.2 0.8 fusion.80
  313.0 1.2 or_select_fusion.2
  314.7 24.7 %all_gather.27 = bf16[32,4096]{1,0:T(8,128)(2,1)S(1)} all-gather(bf16[32,512]{1,0:T(8,128)(2,1)S(1)} %bitcast.89), channel_id=1, replica_groups=mesh['section'=4,'tp'=8] {'tp'}, dimensions={1}, use_global_device_ids=true | all-gather | bytes 294912 | tf_op jit(solution)/shard_map/while/body/eval_jaxpr/all_gather | solution.py:82
  339.4 3.0 fusion.83
  342.4 16.5 %collective-permute-start = (bf16[64,512]{1,0:T(8,128)(2,1)S(1)}, bf16[64,512]{1,0:T(8,128)(2,1)S(1)}, u32[]{:S(2)}, u32[]{:S(2)}) collective-permute-start(bf16[64,512]{1,0:T(8,128)(2,1)S(1)} %maximum_select_fusion.2), channel_id=1, source_target_pairs={{0,8},{8,16},{16,24},{1,9},{9,17},{17,25},{2,10},{10,18},{18,26},{... | collective-permute-start | bytes 196616 | tf_op jit(solution)/shard_map/while/body/eval_jaxpr/ppermute | solution.py:14
  358.9 1.3 collective-permute-done
  360.2 25.4 %all_gather.26 = bf16[64,4096]{1,0:T(8,128)(2,1)S(1)} all-gather(bf16[64,512]{1,0:T(8,128)(2,1)S(1)} %bitcast_select_fusion.3), channel_id=1, replica_groups=mesh['section'=4,'tp'=8] {'tp'}, dimensions={1}, use_global_device_ids=true | all-gather | bytes 589824 | tf_op jit(solution)/shard_map/while/body/eval_jaxpr/all_gather | solution.py:102
  386.6 3.2 fusion.79
  389.8 0.8 fusion.78
  391.5 1.2 or_select_fusion.2
  393.1 25.0 %all_gather.27 = bf16[32,4096]{1,0:T(8,128)(2,1)S(1)} all-gather(bf16[32,512]{1,0:T(8,128)(2,1)S(1)} %bitcast.89), channel_id=1, replica_groups=mesh['section'=4,'tp'=8] {'tp'}, dimensions={1}, use_global_device_ids=true | all-gather | bytes 294912 | tf_op jit(solution)/shard_map/while/body/eval_jaxpr/all_gather | solution.py:82
  418.1 3.0 fusion.83
  421.2 16.4 %collective-permute-start = (bf16[64,512]{1,0:T(8,128)(2,1)S(1)}, bf16[64,512]{1,0:T(8,128)(2,1)S(1)}, u32[]{:S(2)}, u32[]{:S(2)}) collective-permute-start(bf16[64,512]{1,0:T(8,128)(2,1)S(1)} %maximum_select_fusion.2), channel_id=1, source_target_pairs={{0,8},{8,16},{16,24},{1,9},{9,17},{17,25},{2,10},{10,18},{18,26},{... | collective-permute-start | bytes 196616 | tf_op jit(solution)/shard_map/while/body/eval_jaxpr/ppermute | solution.py:14
  437.6 1.3 collective-permute-done
  (86 shorter events, 9.3 us)
Async XLA Ops:
  6.5 38.7 %all-reduce.2.cloned.1.call-start = ((), (), s32[]{:S(2)}) async-start(), calls=%async_computation | async-start | bytes 131072 | tf_op jit(solution)/shard_map/psum | solution.py:36
  7.3 5.7 %copy-start.5 = (bf16[1,4096]{1,0:T(2,128)(2,1)S(1)}, bf16[1,4096]{1,0:T(2,128)(2,1)}, u32[]{:S(2)}) copy-start(bf16[1,4096]{1,0:T(2,128)(2,1)} %param.15) | copy-start | bytes 24580
  7.3 38.0 %copy-start.3 = (bf16[2,32,512]{2,1,0:T(8,128)(2,1)S(1)}, bf16[2,32,512]{2,1,0:T(8,128)(2,1)}, u32[]{:S(2)}) copy-start(bf16[2,32,512]{2,1,0:T(8,128)(2,1)} %param.11) | copy-start | bytes 196612
  7.3 38.8 %copy-start.4 = (s32[2,2]{1,0:T(2,128)S(1)}, s32[2,2]{1,0:T(2,128)}, u32[]{:S(2)}) copy-start(s32[2,2]{1,0:T(2,128)} %param.13) | copy-start | bytes 52
  46.2 30.0 %copy-start = (bf16[4096,512]{1,0:T(8,128)(2,1)S(1)}, bf16[4096,512]{1,0:T(8,128)(2,1)}, u32[]{:S(2)}) copy-start(bf16[4096,512]{1,0:T(8,128)(2,1)} %get-tuple-element.579) | copy-start | bytes 12582916 | tf_op jit(solution)/shard_map/while
  73.0 4.0 copy-start.1
  107.2 17.2 %collective-permute-start = (bf16[64,512]{1,0:T(8,128)(2,1)S(1)}, bf16[64,512]{1,0:T(8,128)(2,1)S(1)}, u32[]{:S(2)}, u32[]{:S(2)}) collective-permute-start(bf16[64,512]{1,0:T(8,128)(2,1)S(1)} %maximum_select_fusion.2), channel_id=1, source_target_pairs={{0,8},{8,16},{16,24},{1,9},{9,17},{17,25},{2,10},{10,18},{18,26},{... | collective-permute-start | bytes 196616 | tf_op jit(solution)/shard_map/while/body/eval_jaxpr/ppermute | solution.py:14
  124.4 30.0 %copy-start = (bf16[4096,512]{1,0:T(8,128)(2,1)S(1)}, bf16[4096,512]{1,0:T(8,128)(2,1)}, u32[]{:S(2)}) copy-start(bf16[4096,512]{1,0:T(8,128)(2,1)} %get-tuple-element.579) | copy-start | bytes 12582916 | tf_op jit(solution)/shard_map/while
  151.2 4.0 copy-start.1
  185.3 17.7 %collective-permute-start = (bf16[64,512]{1,0:T(8,128)(2,1)S(1)}, bf16[64,512]{1,0:T(8,128)(2,1)S(1)}, u32[]{:S(2)}, u32[]{:S(2)}) collective-permute-start(bf16[64,512]{1,0:T(8,128)(2,1)S(1)} %maximum_select_fusion.2), channel_id=1, source_target_pairs={{0,8},{8,16},{16,24},{1,9},{9,17},{17,25},{2,10},{10,18},{18,26},{... | collective-permute-start | bytes 196616 | tf_op jit(solution)/shard_map/while/body/eval_jaxpr/ppermute | solution.py:14
  203.0 29.7 %copy-start = (bf16[4096,512]{1,0:T(8,128)(2,1)S(1)}, bf16[4096,512]{1,0:T(8,128)(2,1)}, u32[]{:S(2)}) copy-start(bf16[4096,512]{1,0:T(8,128)(2,1)} %get-tuple-element.579) | copy-start | bytes 12582916 | tf_op jit(solution)/shard_map/while
  229.6 4.0 copy-start.1
  263.7 17.9 %collective-permute-start = (bf16[64,512]{1,0:T(8,128)(2,1)S(1)}, bf16[64,512]{1,0:T(8,128)(2,1)S(1)}, u32[]{:S(2)}, u32[]{:S(2)}) collective-permute-start(bf16[64,512]{1,0:T(8,128)(2,1)S(1)} %maximum_select_fusion.2), channel_id=1, source_target_pairs={{0,8},{8,16},{16,24},{1,9},{9,17},{17,25},{2,10},{10,18},{18,26},{... | collective-permute-start | bytes 196616 | tf_op jit(solution)/shard_map/while/body/eval_jaxpr/ppermute | solution.py:14
  281.6 29.8 %copy-start = (bf16[4096,512]{1,0:T(8,128)(2,1)S(1)}, bf16[4096,512]{1,0:T(8,128)(2,1)}, u32[]{:S(2)}) copy-start(bf16[4096,512]{1,0:T(8,128)(2,1)} %get-tuple-element.579) | copy-start | bytes 12582916 | tf_op jit(solution)/shard_map/while
  308.2 4.0 copy-start.1
  342.4 17.8 %collective-permute-start = (bf16[64,512]{1,0:T(8,128)(2,1)S(1)}, bf16[64,512]{1,0:T(8,128)(2,1)S(1)}, u32[]{:S(2)}, u32[]{:S(2)}) collective-permute-start(bf16[64,512]{1,0:T(8,128)(2,1)S(1)} %maximum_select_fusion.2), channel_id=1, source_target_pairs={{0,8},{8,16},{16,24},{1,9},{9,17},{17,25},{2,10},{10,18},{18,26},{... | collective-permute-start | bytes 196616 | tf_op jit(solution)/shard_map/while/body/eval_jaxpr/ppermute | solution.py:14
  360.2 29.6 %copy-start = (bf16[4096,512]{1,0:T(8,128)(2,1)S(1)}, bf16[4096,512]{1,0:T(8,128)(2,1)}, u32[]{:S(2)}) copy-start(bf16[4096,512]{1,0:T(8,128)(2,1)} %get-tuple-element.579) | copy-start | bytes 12582916 | tf_op jit(solution)/shard_map/while
  386.6 4.0 copy-start.1
  421.2 17.7 %collective-permute-start = (bf16[64,512]{1,0:T(8,128)(2,1)S(1)}, bf16[64,512]{1,0:T(8,128)(2,1)S(1)}, u32[]{:S(2)}, u32[]{:S(2)}) collective-permute-start(bf16[64,512]{1,0:T(8,128)(2,1)S(1)} %maximum_select_fusion.2), channel_id=1, source_target_pairs={{0,8},{8,16},{16,24},{1,9},{9,17},{17,25},{2,10},{10,18},{18,26},{... | collective-permute-start | bytes 196616 | tf_op jit(solution)/shard_map/while/body/eval_jaxpr/ppermute | solution.py:14
  438.9 0.6 copy-start.2
Sparse Core Ops, SparseCore 0:
  13.1 32.1 all-reduce.1
where the time goes:
time: 447 us; the launch traced here: 446 us
  blocking collectives  252 us (56%)
  starting transfers between devices  81.8 us (18%)
  matrix products  46.6 us (10%)
  waiting for transfers between devices  38.8 us (9%)
  between operations  13.4 us (3%)
  other arithmetic  9.88 us (2%)
    all_gather x5, blocking collectives, advance(): full_rows = lax.all_gather(stream, 'tp', axis=1, tiled=True)  128 us
    all_gather x5, blocking collectives, project_heads(): return add_block(lax.all_gather(head_mix, 'tp', axis=1, tiled=True))  124 us
    ppermute x5, starting transfers between devices, shifted(): return lax.ppermute(block, axis, route)  81.8 us
    psum x1, waiting for transfers between devices, local(): embedded = lax.psum(looked_up.astype(jnp.bfloat16), 'section')  32.2 us
    dot_general x5, matrix products, head_outputs(): jnp.dot(normed, key_weight, preferred_element_type=jnp.float32)  15.9 us
    dot_general x5, matrix products, add_block(): return jnp.dot(piece, out_weight, preferred_element_type=jnp.float32)  15 us
  transfers between devices with their start and end apart: 6, of which 6 were waited for; matrix products, arithmetic and copies ran while one was open for 0% of the time, Pallas kernels for 0%

commit v1 on v0

--- a/solution.py
+++ b/solution.py
@@ -6,6 +6,10 @@
 
 HEADS = 32
 epsilon = 1e-06
+
+
+def read_frames_on_mesh(shard_in):
+    return jnp.sum(lax.all_gather(shard_in, "section"), axis=0)
 
 
 def shifted(block, axis, distance):
@@ -33,7 +37,7 @@
     vocab_cols = lax.broadcasted_iota(jnp.int32, (local_ids.shape[0], vocab_local), 1)
     one_hot = (local_ids[:, None] == vocab_cols).astype(jnp.bfloat16)
     looked_up = jnp.dot(one_hot, embed_table, preferred_element_type=jnp.float32)
-    embedded = lax.psum(looked_up.astype(jnp.bfloat16), "section")
+    embedded = read_frames_on_mesh(looked_up.astype(jnp.bfloat16))
     embedded = embedded.reshape(micro_count, row_count, width_local)
     first_inputs = jnp.concatenate([patches, embedded], axis=1)
     query_pos = lax.broadcasted_iota(jnp.int32, (row_count, 2 * row_count), 0)

time: 447 us -> 407 us (0.911)
  waiting for transfers between devices: 38.8 us -> 6.53 us
  between operations: 13.4 us -> 0.08 us
  blocking collectives: 252 us -> 259 us
    psum x1 -> x0, waiting for transfers between devices: 32.2 us -> none  [local(): embedded = lax.psum(looked_up.astype(jnp.bfloat16), 'section')]
    all_gather x0 -> x1, blocking collectives: none -> 7.07 us  [read_frames_on_mesh(): return jnp.sum(lax.all_gather(shard_in, 'section'), axis=0)]
  transfers between devices with their start and end apart: 6 -> 5, of which waited for: 6 -> 5; matrix products, arithmetic and copies ran while one was open for 0% -> 0% of each run, Pallas kernels for 0% -> 0%
where the time goes in v1:
time: 407 us; the launch traced here: 406 us
  blocking collectives  259 us (64%)
  starting transfers between devices  81.2 us (20%)
  matrix products  46 us (11%)
  other arithmetic  9.29 us (2%)
  waiting for transfers between devices  6.53 us (2%)
  local copies, waits for them, and re-layouts  4.21 us (1%)
    all_gather x5, blocking collectives, advance(): full_rows = lax.all_gather(stream, 'tp', axis=1, tiled=True)  128 us
    all_gather x5, blocking collectives, project_heads(): return add_block(lax.all_gather(head_mix, 'tp', axis=1, tiled=True))  124 us
    ppermute x5, starting transfers between devices, shifted(): return lax.ppermute(block, axis, route)  81.2 us
    dot_general x5, matrix products, head_outputs(): jnp.dot(normed, key_weight, preferred_element_type=jnp.float32)  15.9 us
    dot_general x5, matrix products, add_block(): return jnp.dot(piece, out_weight, preferred_element_type=jnp.float32)  15 us
  transfers between devices with their start and end apart: 5, of which 5 were waited for; matrix products, arithmetic and copies ran while one was open for 0% of the time, Pallas kernels for 0%

profile of v1, /device:TPU:1, one launch (start us, length us, event | category | flops | bytes accessed | tf_op | source)
XLA Modules:
  0.0 406.5 jit_solution(18373605136341013338)
XLA Ops:
  0.8 5.0 %fusion.32 = bf16[64,512]{1,0:T(8,128)(2,1)S(1)} fusion(bf16[8192,512]{1,0:T(8,128)(2,1)} %param.14, s32[64]{0:T(128)S(1)} %sub.33), kind=kOutput, calls=%fused_computation.52 | convolution fusion | flops 537427968 | bytes 8454400 | tf_op jit(solution)/shard_map/dot_general | solution.py:39
  5.8 7.1 %all-gather = bf16[256,512]{1,0:T(8,128)(2,1)S(1)} all-gather(bf16[64,512]{1,0:T(8,128)(2,1)S(1)} %fusion.32), channel_id=2, replica_groups=mesh['section'=4,'tp'=8] {'section'}, dimensions={0}, use_global_device_ids=true | all-gather | bytes 327680 | tf_op jit(solution)/shard_map/all_gather | solution.py:12
  13.0 392.8 %while.19 = (s32[]{:T(128)}, bf16[64,512]{1,0:T(8,128)(2,1)S(1)}, bf16[2,32,512]{2,1,0:T(8,128)(2,1)S(1)}, pred[]{:T(512)}, pred[]{:T(512)}, /*index=5*/s32[]{:T...) while((s32[]{:T(128)}, bf16[64,512]{1,0:T(8,128)(2,1)S(1)}, ...), condition=%wide.region_4.5_spmd.clone.clone, body=%wide.region_1.4_spmd.clone.clone.sunk | while | flops 812038400 | bytes 56055120 | solution.py:115
  13.1 25.7 %all_gather.34 = bf16[64,4096]{1,0:T(8,128)(2,1)S(1)} all-gather(bf16[64,512]{1,0:T(8,128)(2,1)S(1)} %bitcast_select_fusion.3), channel_id=1, replica_groups=mesh['section'=4,'tp'=8] {'tp'}, dimensions={1}, use_global_device_ids=true | all-gather | bytes 589824 | tf_op jit(solution)/shard_map/while/body/eval_jaxpr/all_gather | solution.py:106
  39.9 3.2 fusion.79
  43.1 0.8 fusion.78
  44.0 0.8 fusion.80
  44.8 1.3 or_select_fusion.2
  46.5 24.4 %all_gather.35 = bf16[32,4096]{1,0:T(8,128)(2,1)S(1)} all-gather(bf16[32,512]{1,0:T(8,128)(2,1)S(1)} %bitcast.90), channel_id=1, replica_groups=mesh['section'=4,'tp'=8] {'tp'}, dimensions={1}, use_global_device_ids=true | all-gather | bytes 294912 | tf_op jit(solution)/shard_map/while/body/eval_jaxpr/all_gather | solution.py:86
  70.9 3.0 fusion.83
  73.9 15.8 %collective-permute-start = (bf16[64,512]{1,0:T(8,128)(2,1)S(1)}, bf16[64,512]{1,0:T(8,128)(2,1)S(1)}, u32[]{:S(2)}, u32[]{:S(2)}) collective-permute-start(bf16[64,512]{1,0:T(8,128)(2,1)S(1)} %maximum_select_fusion.2), channel_id=1, source_target_pairs={{0,8},{8,16},{16,24},{1,9},{9,17},{17,25},{2,10},{10,18},{18,26},{... | collective-permute-start | bytes 196616 | tf_op jit(solution)/shard_map/while/body/eval_jaxpr/ppermute | solution.py:18
  89.8 1.3 collective-permute-done
  91.1 25.9 %all_gather.34 = bf16[64,4096]{1,0:T(8,128)(2,1)S(1)} all-gather(bf16[64,512]{1,0:T(8,128)(2,1)S(1)} %bitcast_select_fusion.3), channel_id=1, replica_groups=mesh['section'=4,'tp'=8] {'tp'}, dimensions={1}, use_global_device_ids=true | all-gather | bytes 589824 | tf_op jit(solution)/shard_map/while/body/eval_jaxpr/all_gather | solution.py:106
  118.1 3.2 fusion.79
  121.3 0.8 fusion.78
  122.1 0.8 fusion.80
  122.9 1.3 or_select_fusion.2
  124.6 24.4 %all_gather.35 = bf16[32,4096]{1,0:T(8,128)(2,1)S(1)} all-gather(bf16[32,512]{1,0:T(8,128)(2,1)S(1)} %bitcast.90), channel_id=1, replica_groups=mesh['section'=4,'tp'=8] {'tp'}, dimensions={1}, use_global_device_ids=true | all-gather | bytes 294912 | tf_op jit(solution)/shard_map/while/body/eval_jaxpr/all_gather | solution.py:86
  149.1 3.0 fusion.83
  152.1 16.2 %collective-permute-start = (bf16[64,512]{1,0:T(8,128)(2,1)S(1)}, bf16[64,512]{1,0:T(8,128)(2,1)S(1)}, u32[]{:S(2)}, u32[]{:S(2)}) collective-permute-start(bf16[64,512]{1,0:T(8,128)(2,1)S(1)} %maximum_select_fusion.2), channel_id=1, source_target_pairs={{0,8},{8,16},{16,24},{1,9},{9,17},{17,25},{2,10},{10,18},{18,26},{... | collective-permute-start | bytes 196616 | tf_op jit(solution)/shard_map/while/body/eval_jaxpr/ppermute | solution.py:18
  168.3 1.3 collective-permute-done
  169.6 25.4 %all_gather.34 = bf16[64,4096]{1,0:T(8,128)(2,1)S(1)} all-gather(bf16[64,512]{1,0:T(8,128)(2,1)S(1)} %bitcast_select_fusion.3), channel_id=1, replica_groups=mesh['section'=4,'tp'=8] {'tp'}, dimensions={1}, use_global_device_ids=true | all-gather | bytes 589824 | tf_op jit(solution)/shard_map/while/body/eval_jaxpr/all_gather | solution.py:106
  196.2 3.2 fusion.79
  199.4 0.8 fusion.78
  200.2 0.8 fusion.80
  201.0 1.3 or_select_fusion.2
  202.7 24.9 %all_gather.35 = bf16[32,4096]{1,0:T(8,128)(2,1)S(1)} all-gather(bf16[32,512]{1,0:T(8,128)(2,1)S(1)} %bitcast.90), channel_id=1, replica_groups=mesh['section'=4,'tp'=8] {'tp'}, dimensions={1}, use_global_device_ids=true | all-gather | bytes 294912 | tf_op jit(solution)/shard_map/while/body/eval_jaxpr/all_gather | solution.py:86
  227.6 3.0 fusion.83
  230.6 16.5 %collective-permute-start = (bf16[64,512]{1,0:T(8,128)(2,1)S(1)}, bf16[64,512]{1,0:T(8,128)(2,1)S(1)}, u32[]{:S(2)}, u32[]{:S(2)}) collective-permute-start(bf16[64,512]{1,0:T(8,128)(2,1)S(1)} %maximum_select_fusion.2), channel_id=1, source_target_pairs={{0,8},{8,16},{16,24},{1,9},{9,17},{17,25},{2,10},{10,18},{18,26},{... | collective-permute-start | bytes 196616 | tf_op jit(solution)/shard_map/while/body/eval_jaxpr/ppermute | solution.py:18
  247.2 1.3 collective-permute-done
  248.5 25.5 %all_gather.34 = bf16[64,4096]{1,0:T(8,128)(2,1)S(1)} all-gather(bf16[64,512]{1,0:T(8,128)(2,1)S(1)} %bitcast_select_fusion.3), channel_id=1, replica_groups=mesh['section'=4,'tp'=8] {'tp'}, dimensions={1}, use_global_device_ids=true | all-gather | bytes 589824 | tf_op jit(solution)/shard_map/while/body/eval_jaxpr/all_gather | solution.py:106
  275.1 3.2 fusion.79
  278.3 0.8 fusion.78
  279.1 0.8 fusion.80
  279.9 1.3 or_select_fusion.2
  281.6 24.8 %all_gather.35 = bf16[32,4096]{1,0:T(8,128)(2,1)S(1)} all-gather(bf16[32,512]{1,0:T(8,128)(2,1)S(1)} %bitcast.90), channel_id=1, replica_groups=mesh['section'=4,'tp'=8] {'tp'}, dimensions={1}, use_global_device_ids=true | all-gather | bytes 294912 | tf_op jit(solution)/shard_map/while/body/eval_jaxpr/all_gather | solution.py:86
  306.4 3.0 fusion.83
  309.5 16.2 %collective-permute-start = (bf16[64,512]{1,0:T(8,128)(2,1)S(1)}, bf16[64,512]{1,0:T(8,128)(2,1)S(1)}, u32[]{:S(2)}, u32[]{:S(2)}) collective-permute-start(bf16[64,512]{1,0:T(8,128)(2,1)S(1)} %maximum_select_fusion.2), channel_id=1, source_target_pairs={{0,8},{8,16},{16,24},{1,9},{9,17},{17,25},{2,10},{10,18},{18,26},{... | collective-permute-start | bytes 196616 | tf_op jit(solution)/shard_map/while/body/eval_jaxpr/ppermute | solution.py:18
  325.7 1.3 collective-permute-done
  327.0 25.4 %all_gather.34 = bf16[64,4096]{1,0:T(8,128)(2,1)S(1)} all-gather(bf16[64,512]{1,0:T(8,128)(2,1)S(1)} %bitcast_select_fusion.3), channel_id=1, replica_groups=mesh['section'=4,'tp'=8] {'tp'}, dimensions={1}, use_global_device_ids=true | all-gather | bytes 589824 | tf_op jit(solution)/shard_map/while/body/eval_jaxpr/all_gather | solution.py:106
  353.5 3.2 fusion.79
  356.7 0.8 fusion.78
  357.6 0.8 fusion.80
  358.4 1.3 or_select_fusion.2
  360.0 25.0 %all_gather.35 = bf16[32,4096]{1,0:T(8,128)(2,1)S(1)} all-gather(bf16[32,512]{1,0:T(8,128)(2,1)S(1)} %bitcast.90), channel_id=1, replica_groups=mesh['section'=4,'tp'=8] {'tp'}, dimensions={1}, use_global_device_ids=true | all-gather | bytes 294912 | tf_op jit(solution)/shard_map/while/body/eval_jaxpr/all_gather | solution.py:86
  385.0 3.0 fusion.83
  388.1 16.5 %collective-permute-start = (bf16[64,512]{1,0:T(8,128)(2,1)S(1)}, bf16[64,512]{1,0:T(8,128)(2,1)S(1)}, u32[]{:S(2)}, u32[]{:S(2)}) collective-permute-start(bf16[64,512]{1,0:T(8,128)(2,1)S(1)} %maximum_select_fusion.2), channel_id=1, source_target_pairs={{0,8},{8,16},{16,24},{1,9},{9,17},{17,25},{2,10},{10,18},{18,26},{... | collective-permute-start | bytes 196616 | tf_op jit(solution)/shard_map/while/body/eval_jaxpr/ppermute | solution.py:18
  404.6 1.3 collective-permute-done
  (85 shorter events, 9.0 us)
Async XLA Ops:
  0.8 12.2 %copy-start.3 = (bf16[2,32,512]{2,1,0:T(8,128)(2,1)S(1)}, bf16[2,32,512]{2,1,0:T(8,128)(2,1)}, u32[]{:S(2)}) copy-start(bf16[2,32,512]{2,1,0:T(8,128)(2,1)} %param.11) | copy-start | bytes 196612
  0.8 12.2 %copy-start.5 = (bf16[1,4096]{1,0:T(2,128)(2,1)S(1)}, bf16[1,4096]{1,0:T(2,128)(2,1)}, u32[]{:S(2)}) copy-start(bf16[1,4096]{1,0:T(2,128)(2,1)} %param.15) | copy-start | bytes 24580
  0.8 12.3 %copy-start.4 = (s32[2,2]{1,0:T(2,128)S(1)}, s32[2,2]{1,0:T(2,128)}, u32[]{:S(2)}) copy-start(s32[2,2]{1,0:T(2,128)} %param.13) | copy-start | bytes 52
  13.1 30.1 %copy-start = (bf16[4096,512]{1,0:T(8,128)(2,1)S(1)}, bf16[4096,512]{1,0:T(8,128)(2,1)}, u32[]{:S(2)}) copy-start(bf16[4096,512]{1,0:T(8,128)(2,1)} %get-tuple-element.579) | copy-start | bytes 12582916 | tf_op jit(solution)/shard_map/while
  39.9 4.0 copy-start.1
  73.9 17.1 %collective-permute-start = (bf16[64,512]{1,0:T(8,128)(2,1)S(1)}, bf16[64,512]{1,0:T(8,128)(2,1)S(1)}, u32[]{:S(2)}, u32[]{:S(2)}) collective-permute-start(bf16[64,512]{1,0:T(8,128)(2,1)S(1)} %maximum_select_fusion.2), channel_id=1, source_target_pairs={{0,8},{8,16},{16,24},{1,9},{9,17},{17,25},{2,10},{10,18},{18,26},{... | collective-permute-start | bytes 196616 | tf_op jit(solution)/shard_map/while/body/eval_jaxpr/ppermute | solution.py:18
  91.1 30.2 %copy-start = (bf16[4096,512]{1,0:T(8,128)(2,1)S(1)}, bf16[4096,512]{1,0:T(8,128)(2,1)}, u32[]{:S(2)}) copy-start(bf16[4096,512]{1,0:T(8,128)(2,1)} %get-tuple-element.579) | copy-start | bytes 12582916 | tf_op jit(solution)/shard_map/while
  118.1 4.0 copy-start.1
  152.1 17.5 %collective-permute-start = (bf16[64,512]{1,0:T(8,128)(2,1)S(1)}, bf16[64,512]{1,0:T(8,128)(2,1)S(1)}, u32[]{:S(2)}, u32[]{:S(2)}) collective-permute-start(bf16[64,512]{1,0:T(8,128)(2,1)S(1)} %maximum_select_fusion.2), channel_id=1, source_target_pairs={{0,8},{8,16},{16,24},{1,9},{9,17},{17,25},{2,10},{10,18},{18,26},{... | collective-permute-start | bytes 196616 | tf_op jit(solution)/shard_map/while/body/eval_jaxpr/ppermute | solution.py:18
  169.6 29.7 %copy-start = (bf16[4096,512]{1,0:T(8,128)(2,1)S(1)}, bf16[4096,512]{1,0:T(8,128)(2,1)}, u32[]{:S(2)}) copy-start(bf16[4096,512]{1,0:T(8,128)(2,1)} %get-tuple-element.579) | copy-start | bytes 12582916 | tf_op jit(solution)/shard_map/while
  196.2 4.0 copy-start.1
  230.6 17.8 %collective-permute-start = (bf16[64,512]{1,0:T(8,128)(2,1)S(1)}, bf16[64,512]{1,0:T(8,128)(2,1)S(1)}, u32[]{:S(2)}, u32[]{:S(2)}) collective-permute-start(bf16[64,512]{1,0:T(8,128)(2,1)S(1)} %maximum_select_fusion.2), channel_id=1, source_target_pairs={{0,8},{8,16},{16,24},{1,9},{9,17},{17,25},{2,10},{10,18},{18,26},{... | collective-permute-start | bytes 196616 | tf_op jit(solution)/shard_map/while/body/eval_jaxpr/ppermute | solution.py:18
  248.5 29.8 %copy-start = (bf16[4096,512]{1,0:T(8,128)(2,1)S(1)}, bf16[4096,512]{1,0:T(8,128)(2,1)}, u32[]{:S(2)}) copy-start(bf16[4096,512]{1,0:T(8,128)(2,1)} %get-tuple-element.579) | copy-start | bytes 12582916 | tf_op jit(solution)/shard_map/while
  275.1 4.0 copy-start.1
  309.5 17.5 %collective-permute-start = (bf16[64,512]{1,0:T(8,128)(2,1)S(1)}, bf16[64,512]{1,0:T(8,128)(2,1)S(1)}, u32[]{:S(2)}, u32[]{:S(2)}) collective-permute-start(bf16[64,512]{1,0:T(8,128)(2,1)S(1)} %maximum_select_fusion.2), channel_id=1, source_target_pairs={{0,8},{8,16},{16,24},{1,9},{9,17},{17,25},{2,10},{10,18},{18,26},{... | collective-permute-start | bytes 196616 | tf_op jit(solution)/shard_map/while/body/eval_jaxpr/ppermute | solution.py:18
  327.0 29.7 %copy-start = (bf16[4096,512]{1,0:T(8,128)(2,1)S(1)}, bf16[4096,512]{1,0:T(8,128)(2,1)}, u32[]{:S(2)}) copy-start(bf16[4096,512]{1,0:T(8,128)(2,1)} %get-tuple-element.579) | copy-start | bytes 12582916 | tf_op jit(solution)/shard_map/while
  353.5 4.0 copy-start.1
  388.1 17.8 %collective-permute-start = (bf16[64,512]{1,0:T(8,128)(2,1)S(1)}, bf16[64,512]{1,0:T(8,128)(2,1)S(1)}, u32[]{:S(2)}, u32[]{:S(2)}) collective-permute-start(bf16[64,512]{1,0:T(8,128)(2,1)S(1)} %maximum_select_fusion.2), channel_id=1, source_target_pairs={{0,8},{8,16},{16,24},{1,9},{9,17},{17,25},{2,10},{10,18},{18,26},{... | collective-permute-start | bytes 196616 | tf_op jit(solution)/shard_map/while/body/eval_jaxpr/ppermute | solution.py:18
  405.9 0.6 copy-start.2
